TPU v7x, 256 devices: a whole 4x4x8 slice. The times are simulated.
256 devices in a mesh: depth: 4 (over y), tile: 64 (over x, z, core).
Axes of the slice: x: 4, y: 4, z: 8, core: 2. Of those that a mesh axis runs over, the one named last changes fastest.
Arguments:
- field: float32 [64, 256, 8192], P('depth', None, 'tile'), may hold values from -6 to 6
- light_vectors: float32 [16, 3], replicated, may hold values from -4 to 4
- transfer: float32 [16, 4, 8], replicated, may hold values from 0.05 to 1
- light_index: int32 [4], replicated, may hold values from 0 to 15
- flips: int32 [64], P('tile'), may hold values from 0 to 1
Outputs:
- frames: float32 [4, 4, 256, 8192], P(None, None, 'depth', 'tile')
All inputs are finite; a program needn't handle non-finite values.
Results may differ from a plain program's by a relative error of at most 0.0003.
Values sent between devices are 32-bit elements; how exact they have to be, the bound alone decides.
A program may use at most 128 MiB of HBM per device.

v0:
```python
import functools

import jax
import jax.numpy as jnp
from jax import lax
from jax.experimental import pallas as pl
from jax.experimental.pallas import tpu as pltpu
from jax.sharding import PartitionSpec as P

PASSES = 4
CHANNELS = 4
KNOTS = 8
AMBIENT = 0.3
RANKS = 4
SUB = 8
LANES = 128
SLAB = 16
DEPTH = 64
ROWS = 64
CHUNKS = ROWS // SUB
HALF = SLAB // 2
STEP = 8
PACK = 48
WIDE = 3 * KNOTS * SUB
TALL = PASSES * CHANNELS * SUB
MESH = pl.DeviceIdType.MESH


def rows_at(start):
    return pl.ds(pl.multiple_of(start, SUB), SUB)


def build_weights(lights, transfer, weights):
    sub = lax.broadcasted_iota(jnp.int32, (SUB, KNOTS * SUB), 0)
    lane = lax.broadcasted_iota(jnp.int32, (SUB, KNOTS * SUB), 1)
    knot = lane // SUB
    diagonal = (lane % SUB) == sub
    high, low = [], []
    for p in range(PASSES):
        chosen = lights[p]
        for c in range(CHANNELS):
            line = jnp.zeros((SUB, KNOTS * SUB), jnp.float32)
            for k in range(KNOTS):
                line = jnp.where(knot == k, transfer[chosen, c, k], line)
            if c == CHANNELS - 1:
                line = line * (2.0 / DEPTH)
            line = jnp.where(diagonal, line, 0.0)
            top = line.astype(jnp.bfloat16).astype(jnp.float32)
            high.append(top)
            low.append(line - top)
    high = jnp.concatenate(high, axis=0)
    low = jnp.concatenate(low, axis=0)
    weights[...] = jnp.concatenate([high, low, high], axis=1).astype(jnp.bfloat16)


def pack_borders(tile, tiles, slab, pack, left, right):
    sub = lax.broadcasted_iota(jnp.int32, (SUB, LANES), 0)
    lane = lax.broadcasted_iota(jnp.int32, (SUB, LANES), 1)
    zero = jnp.zeros((SUB, LANES), jnp.float32)
    for rank in range(RANKS):
        base = rank * ROWS
        for part in range(SLAB // SUB):
            above, below = zero, zero
            for s in range(SUB):
                d = part * SUB + s
                if rank > 0:
                    line = slab[d, base - SUB : base, :]
                    above = jnp.where(sub == s, pltpu.roll(line, (s + 1) % SUB, 0), above)
                if rank < RANKS - 1:
                    line = slab[d, base + ROWS : base + ROWS + SUB, :]
                    below = jnp.where(sub == s, pltpu.roll(line, s, 0), below)
            pack[rank, part * SUB : (part + 1) * SUB, :] = above
            pack[rank, SLAB + part * SUB : SLAB + (part + 1) * SUB, :] = below

        def gather(d, carry):
            first, last = carry
            for c in range(CHUNKS):
                place = d * CHUNKS + c
                block = slab[d, base + c * SUB : base + (c + 1) * SUB, :]
                here = lane == place
                first = jnp.where(here, pltpu.roll(block, place, 1), first)
                last = jnp.where(here, pltpu.roll(block, lax.rem(place + 1, LANES), 1), last)
            return first, last

        first, last = lax.fori_loop(0, SLAB, gather, (zero, zero))
        left[rank] = jnp.where(tile == 0, 0.0, first)
        right[rank] = jnp.where(tile == tiles - 1, 0.0, last)


def prepare(chunk, volume, halo, place_ref, nx_ref, ny_ref, nz_ref):
    sub = lax.broadcasted_iota(jnp.int32, (SUB, LANES), 0)
    lane = lax.broadcasted_iota(jnp.int32, (SUB, LANES), 1)
    here = rows_at(SUB + SUB * chunk)
    above = rows_at(SUB * chunk)
    below = rows_at(2 * SUB + SUB * chunk)

    def cells(step, carry):
        for u in range(STEP):
            d = step * STEP + u
            slab = d // SLAB
            place = (d % SLAB) * CHUNKS + chunk
            x = volume[d + 1, here, :]
            dz = volume[d + 2, here, :] - volume[d, here, :]
            up = pltpu.roll(jnp.where(sub == SUB - 1, volume[d + 1, above, :], x), 1, 0)
            down = pltpu.roll(jnp.where(sub == 0, volume[d + 1, below, :], x), SUB - 1, 0)
            dy = down - up
            west = pltpu.roll(halo[slab, 32:40, :], LANES - 1 - place, 1)
            east = pltpu.roll(halo[slab, 40:48, :], lax.rem(LANES - place, LANES), 1)
            prior = pltpu.roll(jnp.where(lane == LANES - 1, west, x), 1, 1)
            after = pltpu.roll(jnp.where(lane == 0, east, x), LANES - 1, 1)
            dx = after - prior
            scale = lax.rsqrt(dx * dx + dy * dy + dz * dz + 4.0)
            nx_ref[d] = dx * scale
            ny_ref[d] = dy * scale
            nz_ref[d] = dz * scale
            place_ref[d] = 3.5 + 3.5 * jnp.tanh(0.5 * x)
        return carry

    lax.fori_loop(0, DEPTH // STEP, cells, 0)


def shade(flip, vectors, weights, place_ref, nx_ref, ny_ref, nz_ref, write):
    start = flip * (DEPTH - 1)
    sign = 1 - 2 * flip
    knots = jnp.concatenate(
        [jnp.full((SUB, LANES), float(k), jnp.float32) for k in range(KNOTS)], axis=0
    )

    def cells(step, state):
        state = list(state)
        at = [start + sign * (step * STEP + u) for u in range(STEP)]
        highs, lows = [], []
        for u in range(STEP):
            place = place_ref[at[u]]
            tent = jnp.maximum(
                0.0, 1.0 - jnp.abs(jnp.concatenate([place] * KNOTS, axis=0) - knots)
            )
            high = tent.astype(jnp.bfloat16)
            lows.append((tent - high.astype(jnp.float32)).astype(jnp.bfloat16))
            highs.append(high)
        for pair in range(STEP // 2):
            a, b = 2 * pair, 2 * pair + 1
            high = jnp.concatenate([highs[a], highs[b]], axis=1)
            low = jnp.concatenate([lows[a], lows[b]], axis=1)
            moving = jnp.concatenate([high, high, low], axis=0)
            mixed = jnp.dot(weights[...], moving, preferred_element_type=jnp.float32)
            for side in range(2):
                u = 2 * pair + side
                nx, ny, nz = nx_ref[at[u]], ny_ref[at[u]], nz_ref[at[u]]
                for p in range(PASSES):
                    channel = [
                        mixed[
                            (p * CHANNELS + c) * SUB : (p * CHANNELS + c + 1) * SUB,
                            side * LANES : (side + 1) * LANES,
                        ]
                        for c in range(CHANNELS)
                    ]
                    lx, ly, lz = vectors[p]
                    bright = AMBIENT + jnp.abs(nx * lx + ny * ly + nz * lz)
                    through = state[p * CHANNELS + 3]
                    taken = through * channel[3]
                    state[p * CHANNELS + 3] = through - taken
                    gain = taken * bright
                    for c in range(3):
                        state[p * CHANNELS + c] = state[p * CHANNELS + c] + gain * channel[c]
        return tuple(state)

    zero = jnp.zeros((SUB, LANES), jnp.float32)
    one = jnp.ones((SUB, LANES), jnp.float32)
    state = lax.fori_loop(
        0, DEPTH // STEP, cells, tuple([zero, zero, zero, one] * PASSES)
    )
    for p in range(PASSES):
        for c in range(3):
            write(p, c, state[p * CHANNELS + c])
        write(p, 3, 1.0 - state[p * CHANNELS + 3])


def kernel(
    tiles,
    flips, lights, light_vectors, transfer, field,
    out,
    slab, volume, pack, left, right, halo, relay, pack_relay, weights,
    place_ref, nx_ref, ny_ref, nz_ref,
    local_sem, col_send, col_recv, pack_send, pack_recv, pack_relay_recv, pack_forward,
    near_send, near_recv, far_send, far_recv, hop_send, hop_recv,
):
    rank = lax.axis_index("depth")
    tile = lax.axis_index("tile")
    ahead, behind = (rank + 1) % RANKS, (rank + RANKS - 1) % RANKS
    across = (rank + 2) % RANKS
    sides = (ahead, behind)
    east, west = (tile + 1) % tiles, (tile + tiles - 1) % tiles

    fetch = pltpu.make_async_copy(field, slab, local_sem.at[0])
    fetch.start()
    own = pltpu.make_async_copy(
        field.at[:, pl.ds(pl.multiple_of(rank * ROWS, SUB), ROWS), :],
        volume.at[pl.ds(1 + rank * SLAB, SLAB), pl.ds(SUB, ROWS), :],
        local_sem.at[1],
    )
    own.start()

    barrier = pltpu.get_barrier_semaphore()
    for where in sides:
        pl.semaphore_signal(barrier, inc=1, device_id=(where, tile), device_id_type=MESH)
    for where in (east, west):
        pl.semaphore_signal(barrier, inc=1, device_id=(rank, where), device_id_type=MESH)
    pl.semaphore_wait(barrier, 4)

    def near(side, c):
        return pltpu.make_async_remote_copy(
            src_ref=field.at[:, rows_at(sides[side] * ROWS + c * SUB), :],
            dst_ref=volume.at[pl.ds(1 + rank * SLAB, SLAB), rows_at(SUB + c * SUB), :],
            send_sem=near_send.at[side, c],
            recv_sem=near_recv.at[side, c],
            device_id=(sides[side], tile),
            device_id_type=MESH,
        )

    def far(side, c):
        return pltpu.make_async_remote_copy(
            src_ref=field.at[pl.ds(side * HALF, HALF), rows_at(across * ROWS + c * SUB), :],
            dst_ref=relay.at[side, c],
            send_sem=far_send.at[side, c],
            recv_sem=far_recv.at[side, c],
            device_id=(sides[side], tile),
            device_id_type=MESH,
        )

    def hop(side, c):
        origin = sides[1 - side]
        return pltpu.make_async_remote_copy(
            src_ref=relay.at[side, c],
            dst_ref=volume.at[
                pl.ds(1 + origin * SLAB + side * HALF, HALF), rows_at(SUB + c * SUB), :
            ],
            send_sem=hop_send.at[side, c],
            recv_sem=hop_recv.at[side, c],
            device_id=(sides[side], tile),
            device_id_type=MESH,
        )

    for side in range(2):
        far(side, 0).start()
    for side in range(2):
        far(side, 1).start()
    for side in range(2):
        near(side, 0).start()

    zero_layer = jnp.zeros((ROWS + 2 * SUB, LANES), jnp.float32)
    volume[0] = zero_layer
    volume[DEPTH + 1] = zero_layer
    fetch.wait()
    pack_borders(tile, tiles, slab, pack, left, right)
    build_weights(lights, transfer, weights)

    columns = [
        pltpu.make_async_remote_copy(
            src_ref=source,
            dst_ref=pack.at[:, pl.ds(start, SUB), :],
            send_sem=col_send.at[n],
            recv_sem=col_recv.at[n],
            device_id=(rank, where),
            device_id_type=MESH,
        )
        for n, (source, start, where) in enumerate(((right, 32, east), (left, 40, west)))
    ]
    for copy in columns:
        copy.start()
    own.wait()
    for copy in columns:
        copy.wait_recv()

    packs = [
        pltpu.make_async_remote_copy(
            src_ref=pack.at[sides[side]],
            dst_ref=halo.at[rank],
            send_sem=pack_send.at[side],
            recv_sem=pack_recv.at[side],
            device_id=(sides[side], tile),
            device_id_type=MESH,
        )
        for side in range(2)
    ]
    packs.append(
        pltpu.make_async_remote_copy(
            src_ref=pack.at[across],
            dst_ref=pack_relay,
            send_sem=pack_send.at[2],
            recv_sem=pack_relay_recv,
            device_id=(ahead, tile),
            device_id_type=MESH,
        )
    )
    packs[2].start()
    packs[0].start()
    packs[1].start()
    mine = pltpu.make_async_copy(pack.at[rank], halo.at[rank], local_sem.at[2])
    mine.start()
    packs[2].wait_recv()
    forward = pltpu.make_async_remote_copy(
        src_ref=pack_relay,
        dst_ref=halo.at[behind],
        send_sem=pack_forward.at[0],
        recv_sem=pack_forward.at[1],
        device_id=(ahead, tile),
        device_id_type=MESH,
    )
    forward.start()
    mine.wait()
    packs[0].wait_recv()
    packs[1].wait_recv()
    forward.wait_recv()

    def expand(d, carry):
        source = d // SLAB
        line = d % SLAB
        volume[d + 1, 0:SUB, :] = jnp.broadcast_to(halo[source, pl.ds(line, 1), :], (SUB, LANES))
        volume[d + 1, SUB + ROWS : ROWS + 2 * SUB, :] = jnp.broadcast_to(
            halo[source, pl.ds(SLAB + line, 1), :], (SUB, LANES)
        )
        return carry

    lax.fori_loop(0, DEPTH, expand, 0)

    flip = flips[0]
    vectors = [[light_vectors[lights[p], a] for a in range(3)] for p in range(PASSES)]

    def compute(chunk):
        prepare(chunk, volume, halo, place_ref, nx_ref, ny_ref, nz_ref)

        def write(p, c, value):
            out[p, c, rows_at(chunk * SUB), :] = value

        shade(flip, vectors, weights, place_ref, nx_ref, ny_ref, nz_ref, write)

    def advance(c, carry):
        @pl.when(c < CHUNKS)
        def _():
            for side in range(2):
                far(side, c).wait_recv()
                hop(side, c).start()

        @pl.when(c < CHUNKS - 2)
        def _():
            for side in range(2):
                far(side, c + 2).start()

        @pl.when(c < CHUNKS - 1)
        def _():
            for side in range(2):
                near(side, c + 1).start()

        @pl.when(c < CHUNKS)
        def _():
            for side in range(2):
                near(side, c).wait_recv()
                hop(side, c).wait_recv()

        @pl.when(c > 0)
        def _():
            compute(c - 1)

        return carry

    lax.fori_loop(0, CHUNKS + 1, advance, 0)

    def drain(c, carry):
        for side in range(2):
            near(side, c).wait_send()
            far(side, c).wait_send()
            hop(side, c).wait_send()
        return carry

    lax.fori_loop(0, CHUNKS, drain, 0)
    for copy in columns + packs + [forward]:
        copy.wait_send()


def solution(mesh):
    tiles = mesh.shape["tile"]

    def on_device(field, light_vectors, transfer, light_index, flips):
        smem = pl.BlockSpec(memory_space=pltpu.SMEM)
        vmem = pl.BlockSpec(memory_space=pltpu.VMEM)
        dma = pltpu.SemaphoreType.DMA
        f32 = jnp.float32
        return pl.pallas_call(
            functools.partial(kernel, tiles),
            out_shape=jax.ShapeDtypeStruct((PASSES, CHANNELS, ROWS, LANES), f32),
            in_specs=[smem, smem, smem, smem, pl.BlockSpec(memory_space=pl.ANY)],
            out_specs=vmem,
            scratch_shapes=[
                pltpu.VMEM((SLAB, RANKS * ROWS, LANES), f32),
                pltpu.VMEM((DEPTH + 2, ROWS + 2 * SUB, LANES), f32),
                pltpu.VMEM((RANKS, PACK, LANES), f32),
                pltpu.VMEM((RANKS, SUB, LANES), f32),
                pltpu.VMEM((RANKS, SUB, LANES), f32),
                pltpu.VMEM((RANKS, PACK, LANES), f32),
                pltpu.VMEM((2, CHUNKS, HALF, SUB, LANES), f32),
                pltpu.VMEM((PACK, LANES), f32),
                pltpu.VMEM((TALL, WIDE), jnp.bfloat16),
                pltpu.VMEM((DEPTH, SUB, LANES), f32),
                pltpu.VMEM((DEPTH, SUB, LANES), f32),
                pltpu.VMEM((DEPTH, SUB, LANES), f32),
                pltpu.VMEM((DEPTH, SUB, LANES), f32),
                dma((3,)), dma((2,)), dma((2,)), dma((3,)), dma((2,)), dma, dma((2,)),
                dma((2, CHUNKS)), dma((2, CHUNKS)), dma((2, CHUNKS)),
                dma((2, CHUNKS)), dma((2, CHUNKS)), dma((2, CHUNKS)),
            ],
            compiler_params=pltpu.CompilerParams(collective_id=0, has_side_effects=True),
            name="render",
        )(flips, light_index, light_vectors, transfer, field)

    in_specs = (P("depth", None, "tile"), P(), P(), P(), P("tile"))
    out_specs = P(None, None, "depth", "tile")
    return jax.shard_map(
        on_device, mesh=mesh, in_specs=in_specs, out_specs=out_specs, check_vma=False
    )
```

profile of v0, /device:TPU:8, one launch (start us, length us, event | category | flops | bytes accessed | tf_op | source)
XLA Modules:
  0.0 89.8 jit_solution(4322513552230966082)
XLA Ops:
  0.7 1.4 %copy.6.light_vectors = f32[16,3]{1,0:T(8,128)} copy(f32[16,3]{0,1:T(4,128)} %param.6) | data formatting | bytes 384 | tf_op args[1]
  2.0 1.4 %copy.7.transfer = f32[16,4,8]{2,1,0:T(4,128)} copy(f32[16,4,8]{0,2,1:T(8,128)} %param.7) | data formatting | bytes 4096 | tf_op args[2]
  3.4 84.5 %render.1 = f32[4,4,64,128]{3,2,1,0:T(8,128)} custom-call(s32[1]{0:T(128)S(6)} %copy.9.flips, s32[4]{0:T(128)} %lights.1, f32[16,3]{1,0:T(8,128)} %copy.6.light_vectors, f32[16,4,8]{2,1,0:T(4,128)} %copy.7.transfer, f32[16,256,128]{2,1,0:T(8,128)} %field.1), custom_call_target="tpu_custom_call" | custom-call | tf_op jit(solution)/shard_map/render/pallas_call | solution.py:389
  87.9 1.9 %copy.10 = f32[4,4,64,128]{3,2,1,0:T(8,128)} copy(f32[4,4,64,128]{3,2,1,0:T(8,128)} %render.1) | data formatting | bytes 1048576
where the time goes:
time: 90.2 us; the launch traced here: 89.8 us
  Pallas kernels  84.5 us (94%)
  local copies, waits for them, and re-layouts  4.64 us (5%)
    pallas_call x1, Pallas kernels, on_device(): pl.pallas_call(functools.partial(kernel, tiles), out_shape=jax.ShapeDtype...  84.5 us
    unnamed x3, local copies, waits for them, and re-layouts  4.64 us

commit v1 on v0

--- a/solution.py
+++ b/solution.py
@@ -19,10 +19,16 @@
 ROWS = 64
 CHUNKS = ROWS // SUB
 HALF = SLAB // 2
-STEP = 8
+STEP = 64
 PACK = 48
-WIDE = 3 * KNOTS * SUB
-TALL = PASSES * CHANNELS * SUB
+TWO = 2 * SUB
+FINE = 32.0
+SPAN = 0.5 * (KNOTS - 1) * FINE
+SLOTS = KNOTS - 1 + 3
+OUTPUTS = CHANNELS + 1
+WIDE = (3 * SLOTS + 2) * SUB
+TALL = PASSES * OUTPUTS * SUB
+STAGED = 4
 MESH = pl.DeviceIdType.MESH
 
 
@@ -30,33 +36,54 @@
     return pl.ds(pl.multiple_of(start, SUB), SUB)
 
 
-def build_weights(lights, transfer, weights):
-    sub = lax.broadcasted_iota(jnp.int32, (SUB, KNOTS * SUB), 0)
-    lane = lax.broadcasted_iota(jnp.int32, (SUB, KNOTS * SUB), 1)
-    knot = lane // SUB
+def build_weights(lights, vectors, transfer, weights):
+    sub = lax.broadcasted_iota(jnp.int32, (SUB, WIDE), 0)
+    lane = lax.broadcasted_iota(jnp.int32, (SUB, WIDE), 1)
+    slot = lane // SUB
     diagonal = (lane % SUB) == sub
-    high, low = [], []
+    constant = slot >= 3 * SLOTS
+    item = jnp.where(constant, SLOTS, slot % SLOTS)
+    is_low = ((slot >= SLOTS) & (slot < 2 * SLOTS)) | (slot == 3 * SLOTS + 1)
     for p in range(PASSES):
         chosen = lights[p]
-        for c in range(CHANNELS):
-            line = jnp.zeros((SUB, KNOTS * SUB), jnp.float32)
-            for k in range(KNOTS):
-                line = jnp.where(knot == k, transfer[chosen, c, k], line)
-            if c == CHANNELS - 1:
-                line = line * (2.0 / DEPTH)
+        for c in range(OUTPUTS):
+            line = jnp.zeros((SUB, WIDE), jnp.float32)
+            if c < CHANNELS:
+                scale = 2.0 / DEPTH if c == CHANNELS - 1 else 1.0
+                values = [transfer[c, k, chosen] * scale for k in range(KNOTS)]
+                for k in range(KNOTS - 1):
+                    line = jnp.where(item == k, (values[k + 1] - values[k]) * (1.0 / FINE), line)
+                line = jnp.where(item == SLOTS, values[0], line)
+            else:
+                for n, axis in enumerate((2, 0, 1)):
+                    line = jnp.where(item == KNOTS - 1 + n, vectors[axis, chosen], line)
             line = jnp.where(diagonal, line, 0.0)
-            top = line.astype(jnp.bfloat16).astype(jnp.float32)
-            high.append(top)
-            low.append(line - top)
-    high = jnp.concatenate(high, axis=0)
-    low = jnp.concatenate(low, axis=0)
-    weights[...] = jnp.concatenate([high, low, high], axis=1).astype(jnp.bfloat16)
+            high = line.astype(jnp.bfloat16).astype(jnp.float32)
+            start = (p * OUTPUTS + c) * SUB
+            staged = jnp.where(is_low, line - high, high)
+            weights[start : start + SUB, :] = staged
 
 
 def pack_borders(tile, tiles, slab, pack, left, right):
     sub = lax.broadcasted_iota(jnp.int32, (SUB, LANES), 0)
     lane = lax.broadcasted_iota(jnp.int32, (SUB, LANES), 1)
     zero = jnp.zeros((SUB, LANES), jnp.float32)
+
+    def gather(rank, carry):
+        base = rank * ROWS
+        first, last = [zero] * 2, [zero] * 2
+        for d in range(SLAB):
+            for c in range(CHUNKS):
+                place = d * CHUNKS + c
+                block = slab[d, pl.ds(pl.multiple_of(base + c * SUB, SUB), SUB), :]
+                here = lane == place
+                first[c % 2] = jnp.where(here, pltpu.roll(block, place, 1) if place else block, first[c % 2])
+                last[c % 2] = jnp.where(here, pltpu.roll(block, place + 1, 1) if place < LANES - 1 else block, last[c % 2])
+        left[rank] = jnp.where(tile == 0, 0.0, first[0] + first[1])
+        right[rank] = jnp.where(tile == tiles - 1, 0.0, last[0] + last[1])
+        return carry
+
+    lax.fori_loop(0, RANKS, gather, 0)
     for rank in range(RANKS):
         base = rank * ROWS
         for part in range(SLAB // SUB):
@@ -72,104 +99,137 @@
             pack[rank, part * SUB : (part + 1) * SUB, :] = above
             pack[rank, SLAB + part * SUB : SLAB + (part + 1) * SUB, :] = below
 
-        def gather(d, carry):
-            first, last = carry
-            for c in range(CHUNKS):
-                place = d * CHUNKS + c
-                block = slab[d, base + c * SUB : base + (c + 1) * SUB, :]
-                here = lane == place
-                first = jnp.where(here, pltpu.roll(block, place, 1), first)
-                last = jnp.where(here, pltpu.roll(block, lax.rem(place + 1, LANES), 1), last)
-            return first, last
-
-        first, last = lax.fori_loop(0, SLAB, gather, (zero, zero))
-        left[rank] = jnp.where(tile == 0, 0.0, first)
-        right[rank] = jnp.where(tile == tiles - 1, 0.0, last)
-
-
-def prepare(chunk, volume, halo, place_ref, nx_ref, ny_ref, nz_ref):
-    sub = lax.broadcasted_iota(jnp.int32, (SUB, LANES), 0)
+
+def pair(a, b):
+    return jnp.concatenate([a, b], axis=0).astype(jnp.float32).astype(jnp.bfloat16)
+
+
+def build_shift(shift):
+    lane = lax.broadcasted_iota(jnp.int32, (LANES, LANES), 0)
+    out = lax.broadcasted_iota(jnp.int32, (LANES, LANES), 1)
+    inner = jnp.where(lane == out + 1, 1.0, jnp.where(lane == out - 1, -1.0, 0.0))
+    place = lane % CHUNKS
+    outer = jnp.where(
+        (out == LANES - 1) & (place == 0), 1.0, jnp.where((out == 0) & (place == 1), -1.0, 0.0)
+    )
+    for n, part in enumerate((inner, inner, outer, outer)):
+        shift[n * LANES : (n + 1) * LANES, :] = part.astype(jnp.bfloat16)
+
+
+def prepare(chunk, volume, halo, shift, stage):
     lane = lax.broadcasted_iota(jnp.int32, (SUB, LANES), 1)
+    bf16 = jnp.bfloat16
+    first = lane % CHUNKS == 0
+    couple = pair(lane // 2, lane // 2)
+    nothing = jnp.zeros((TWO, LANES), bf16)
     here = rows_at(SUB + SUB * chunk)
-    above = rows_at(SUB * chunk)
-    below = rows_at(2 * SUB + SUB * chunk)
-
-    def cells(step, carry):
-        for u in range(STEP):
-            d = step * STEP + u
-            slab = d // SLAB
-            place = (d % SLAB) * CHUNKS + chunk
-            x = volume[d + 1, here, :]
+    above = pl.ds(SUB + SUB * chunk - 1, SUB)
+    below = pl.ds(SUB + SUB * chunk + 1, SUB)
+    for source in range(RANKS):
+        west = pltpu.roll(halo[source, 32:40, :], (LANES + 1 - chunk) % LANES, 1)
+        east = pltpu.roll(halo[source, 40:48, :], (LANES - chunk) % LANES, 1)
+        border = jnp.where(first, east, west)
+        border_top = pair(border, border)
+        rest = border - border_top[:SUB].astype(jnp.float32)
+        border_low = pair(rest, rest)
+        rows = []
+        for two in range(SLAB // 2):
+            d = source * SLAB + 2 * two
+            x = jnp.concatenate([volume[d + 1, here, :], volume[d + 2, here, :]], axis=0)
+            top = x.astype(bf16)
+            low = (x - top.astype(jnp.float32)).astype(bf16)
+            wanted = jnp.concatenate(
+                [jnp.full((SUB, LANES), float((2 * two + n) * CHUNKS // 2), jnp.float32) for n in range(2)],
+                axis=0,
+            ).astype(bf16)
+            mask = couple == wanted
+            rows.append(
+                jnp.concatenate(
+                    [top, low, jnp.where(mask, border_top, nothing), jnp.where(mask, border_low, nothing)],
+                    axis=1,
+                )
+            )
+        across = jnp.dot(
+            jnp.concatenate(rows, axis=0), shift[...], preferred_element_type=jnp.float32
+        )
+        for u in range(SLAB):
+            d = source * SLAB + u
+            dx = across[u * SUB : (u + 1) * SUB, :]
             dz = volume[d + 2, here, :] - volume[d, here, :]
-            up = pltpu.roll(jnp.where(sub == SUB - 1, volume[d + 1, above, :], x), 1, 0)
-            down = pltpu.roll(jnp.where(sub == 0, volume[d + 1, below, :], x), SUB - 1, 0)
-            dy = down - up
-            west = pltpu.roll(halo[slab, 32:40, :], LANES - 1 - place, 1)
-            east = pltpu.roll(halo[slab, 40:48, :], lax.rem(LANES - place, LANES), 1)
-            prior = pltpu.roll(jnp.where(lane == LANES - 1, west, x), 1, 1)
-            after = pltpu.roll(jnp.where(lane == 0, east, x), LANES - 1, 1)
-            dx = after - prior
+            dy = volume[d + 1, below, :] - volume[d + 1, above, :]
             scale = lax.rsqrt(dx * dx + dy * dy + dz * dz + 4.0)
-            nx_ref[d] = dx * scale
-            ny_ref[d] = dy * scale
-            nz_ref[d] = dz * scale
-            place_ref[d] = 3.5 + 3.5 * jnp.tanh(0.5 * x)
-        return carry
-
-    lax.fori_loop(0, DEPTH // STEP, cells, 0)
-
-
-def shade(flip, vectors, weights, place_ref, nx_ref, ny_ref, nz_ref, write):
+            stage[d, 0] = SPAN + SPAN * jnp.tanh(0.5 * volume[d + 1, here, :])
+            stage[d, 1] = dx * scale
+            stage[d, 2] = dy * scale
+            stage[d, 3] = dz * scale
+
+
+def shade(flip, weights, stage, write):
     start = flip * (DEPTH - 1)
     sign = 1 - 2 * flip
-    knots = jnp.concatenate(
-        [jnp.full((SUB, LANES), float(k), jnp.float32) for k in range(KNOTS)], axis=0
-    )
+    bf16 = jnp.bfloat16
+
+    def levels(values):
+        return jnp.concatenate([jnp.full((SUB, LANES), float(v), jnp.float32) for v in values], axis=0).astype(bf16)
+
+    none = jnp.zeros((SUB, LANES), jnp.float32)
+    fine_ones = jnp.full((SUB, LANES), FINE, jnp.float32)
+    base = [levels((FINE * 2 * n, FINE * (2 * n + 1))) for n in range(4)]
+    index = [levels((2 * n, 2 * n + 1 if n < 3 else 99)) for n in range(4)]
+    zero2 = levels((0, 0))
+    full2 = levels((FINE, FINE))
+    ones = levels((1, 1))
 
     def cells(step, state):
         state = list(state)
-        at = [start + sign * (step * STEP + u) for u in range(STEP)]
-        highs, lows = [], []
+        columns = []
         for u in range(STEP):
-            place = place_ref[at[u]]
-            tent = jnp.maximum(
-                0.0, 1.0 - jnp.abs(jnp.concatenate([place] * KNOTS, axis=0) - knots)
-            )
-            high = tent.astype(jnp.bfloat16)
-            lows.append((tent - high.astype(jnp.float32)).astype(jnp.bfloat16))
-            highs.append(high)
-        for pair in range(STEP // 2):
-            a, b = 2 * pair, 2 * pair + 1
-            high = jnp.concatenate([highs[a], highs[b]], axis=1)
-            low = jnp.concatenate([lows[a], lows[b]], axis=1)
-            moving = jnp.concatenate([high, high, low], axis=0)
+            at = start + sign * (step * STEP + u)
+            place, nx, ny, nz = [stage[at, n] for n in range(STAGED)]
+            level = jnp.floor(place)
+            step_in = place - level
+            floor_knot = jnp.floor(level * (1.0 / FINE))
+            whole, rest, knot = pair(level, level), pair(step_in, step_in), pair(floor_knot, floor_knot)
+            flat, deep, deep_full = pair(nx, ny), pair(none, nz), pair(fine_ones, nz)
+            flat_top, deep_top = flat.astype(jnp.float32), deep.astype(jnp.float32)
+            flat_low = pair(nx - flat_top[:SUB], ny - flat_top[SUB:])
+            deep_low = pair(none, nz - deep_top[SUB:])
+            ramp = [
+                jnp.minimum(
+                    jnp.maximum(whole - base[n], zero2 if n < 3 else deep),
+                    full2 if n < 3 else deep_full,
+                )
+                for n in range(4)
+            ]
+            fine = [
+                jnp.where(knot == index[n], rest, zero2 if n < 3 else deep_low) for n in range(4)
+            ]
+            top = ramp + [flat]
+            columns.append(jnp.concatenate(top + top + fine + [flat_low, ones], axis=0))
+        for two in range(STEP // 2):
+            moving = jnp.concatenate(columns[2 * two : 2 * two + 2], axis=1)
             mixed = jnp.dot(weights[...], moving, preferred_element_type=jnp.float32)
             for side in range(2):
-                u = 2 * pair + side
-                nx, ny, nz = nx_ref[at[u]], ny_ref[at[u]], nz_ref[at[u]]
                 for p in range(PASSES):
-                    channel = [
+                    red, green, blue, opacity, facing = [
                         mixed[
-                            (p * CHANNELS + c) * SUB : (p * CHANNELS + c + 1) * SUB,
+                            (p * OUTPUTS + c) * SUB : (p * OUTPUTS + c + 1) * SUB,
                             side * LANES : (side + 1) * LANES,
                         ]
-                        for c in range(CHANNELS)
+                        for c in range(OUTPUTS)
                     ]
-                    lx, ly, lz = vectors[p]
-                    bright = AMBIENT + jnp.abs(nx * lx + ny * ly + nz * lz)
+                    bright = AMBIENT + jnp.abs(facing)
                     through = state[p * CHANNELS + 3]
-                    taken = through * channel[3]
+                    taken = through * opacity
                     state[p * CHANNELS + 3] = through - taken
                     gain = taken * bright
-                    for c in range(3):
-                        state[p * CHANNELS + c] = state[p * CHANNELS + c] + gain * channel[c]
+                    for c, channel in enumerate((red, green, blue)):
+                        state[p * CHANNELS + c] = state[p * CHANNELS + c] + gain * channel
         return tuple(state)
 
     zero = jnp.zeros((SUB, LANES), jnp.float32)
     one = jnp.ones((SUB, LANES), jnp.float32)
-    state = lax.fori_loop(
-        0, DEPTH // STEP, cells, tuple([zero, zero, zero, one] * PASSES)
-    )
+    state = cells(0, tuple([zero, zero, zero, one] * PASSES))
     for p in range(PASSES):
         for c in range(3):
             write(p, c, state[p * CHANNELS + c])
@@ -180,8 +240,7 @@
     tiles,
     flips, lights, light_vectors, transfer, field,
     out,
-    slab, volume, pack, left, right, halo, relay, pack_relay, weights,
-    place_ref, nx_ref, ny_ref, nz_ref,
+    slab, volume, pack, left, right, halo, relay, pack_relay, draft, weights, shift, stage,
     local_sem, col_send, col_recv, pack_send, pack_recv, pack_relay_recv, pack_forward,
     near_send, near_recv, far_send, far_recv, hop_send, hop_recv,
 ):
@@ -241,10 +300,12 @@
             device_id_type=MESH,
         )
 
-    for side in range(2):
-        far(side, 0).start()
-    for side in range(2):
-        far(side, 1).start()
+    def launch(c, carry):
+        for side in range(2):
+            far(side, c).start()
+        return carry
+
+    lax.fori_loop(0, CHUNKS, launch, 0)
     for side in range(2):
         near(side, 0).start()
 
@@ -253,7 +314,9 @@
     volume[DEPTH + 1] = zero_layer
     fetch.wait()
     pack_borders(tile, tiles, slab, pack, left, right)
-    build_weights(lights, transfer, weights)
+    build_weights(lights, light_vectors, transfer, draft)
+    weights[...] = draft[...].astype(jnp.bfloat16)
+    build_shift(shift)
 
     columns = [
         pltpu.make_async_remote_copy(
@@ -325,32 +388,31 @@
     lax.fori_loop(0, DEPTH, expand, 0)
 
     flip = flips[0]
-    vectors = [[light_vectors[lights[p], a] for a in range(3)] for p in range(PASSES)]
 
     def compute(chunk):
-        prepare(chunk, volume, halo, place_ref, nx_ref, ny_ref, nz_ref)
+        prepare(chunk, volume, halo, shift, stage)
 
         def write(p, c, value):
             out[p, c, rows_at(chunk * SUB), :] = value
 
-        shade(flip, vectors, weights, place_ref, nx_ref, ny_ref, nz_ref, write)
+        shade(flip, weights, stage, write)
+
+    def relay_on(c):
+        for side in range(2):
+            far(side, c).wait_recv()
+            hop(side, c).start()
+
+    relay_on(0)
+    relay_on(1)
+    for side in range(2):
+        near(side, 1).start()
 
     def advance(c, carry):
-        @pl.when(c < CHUNKS)
-        def _():
-            for side in range(2):
-                far(side, c).wait_recv()
-                hop(side, c).start()
-
         @pl.when(c < CHUNKS - 2)
         def _():
+            relay_on(c + 2)
             for side in range(2):
-                far(side, c + 2).start()
-
-        @pl.when(c < CHUNKS - 1)
-        def _():
-            for side in range(2):
-                near(side, c + 1).start()
+                near(side, c + 2).start()
 
         @pl.when(c < CHUNKS)
         def _():
@@ -400,18 +462,17 @@
                 pltpu.VMEM((RANKS, PACK, LANES), f32),
                 pltpu.VMEM((2, CHUNKS, HALF, SUB, LANES), f32),
                 pltpu.VMEM((PACK, LANES), f32),
+                pltpu.VMEM((TALL, WIDE), f32),
                 pltpu.VMEM((TALL, WIDE), jnp.bfloat16),
-                pltpu.VMEM((DEPTH, SUB, LANES), f32),
-                pltpu.VMEM((DEPTH, SUB, LANES), f32),
-                pltpu.VMEM((DEPTH, SUB, LANES), f32),
-                pltpu.VMEM((DEPTH, SUB, LANES), f32),
+                pltpu.VMEM((4 * LANES, LANES), jnp.bfloat16),
+                pltpu.VMEM((DEPTH, STAGED, SUB, LANES), f32),
                 dma((3,)), dma((2,)), dma((2,)), dma((3,)), dma((2,)), dma, dma((2,)),
                 dma((2, CHUNKS)), dma((2, CHUNKS)), dma((2, CHUNKS)),
                 dma((2, CHUNKS)), dma((2, CHUNKS)), dma((2, CHUNKS)),
             ],
             compiler_params=pltpu.CompilerParams(collective_id=0, has_side_effects=True),
             name="render",
-        )(flips, light_index, light_vectors, transfer, field)
+        )(flips, light_index, light_vectors.T, jnp.transpose(transfer, (1, 2, 0)), field)
 
     in_specs = (P("depth", None, "tile"), P(), P(), P(), P("tile"))
     out_specs = P(None, None, "depth", "tile")

time: 90.2 us -> 44.6 us (0.49)
  Pallas kernels: 84.5 us -> 41.9 us
  local copies, waits for them, and re-layouts: 4.64 us -> 1.89 us
    pallas_call x1, Pallas kernels: 84.5 us -> 41.9 us  [on_device(): pl.pallas_call(functools.partial(kernel, tiles), out_shape=jax.ShapeDtype...]
    unnamed x3 -> x1, local copies, waits for them, and re-layouts: 4.64 us -> 1.89 us
where the time goes in v1:
time: 44.6 us; the launch traced here: 44.4 us
  Pallas kernels  41.9 us (94%)
  local copies, waits for them, and re-layouts  1.89 us (4%)
  between operations  0.66 us (1%)
    pallas_call x1, Pallas kernels, on_device(): pl.pallas_call(functools.partial(kernel, tiles), out_shape=jax.ShapeDtype...  41.9 us
    unnamed x1, local copies, waits for them, and re-layouts  1.89 us

profile of v1, /device:TPU:8, one launch (start us, length us, event | category | flops | bytes accessed | tf_op | source)
XLA Modules:
  0.0 44.4 jit_solution(17429231757972412040)
XLA Ops:
  0.7 41.9 %render.1 = f32[4,4,64,128]{3,2,1,0:T(8,128)} custom-call(s32[1]{0:T(128)S(6)} %copy.7.flips, s32[4]{0:T(128)} %lights.1, f32[3,16]{1,0:T(4,128)} %bitcast.3, f32[4,8,16]{2,1,0:T(8,128)} %bitcast.2, f32[16,256,128]{2,1,0:T(8,128)} %field.1), custom_call_target="tpu_custom_call" | custom-call | tf_op jit(solution)/shard_map/render/pallas_call | solution.py:451
  42.5 1.9 %copy.8 = f32[4,4,64,128]{3,2,1,0:T(8,128)} copy(f32[4,4,64,128]{3,2,1,0:T(8,128)} %render.1) | data formatting | bytes 1048576

commit v2 on v1

--- a/solution.py
+++ b/solution.py
@@ -20,7 +20,10 @@
 CHUNKS = ROWS // SUB
 HALF = SLAB // 2
 STEP = 64
-PACK = 48
+PACK = 64
+LAST = CHUNKS - 1
+MIDDLE = 48
+TOTAL = ROWS + 3 * SUB
 TWO = 2 * SUB
 FINE = 32.0
 SPAN = 0.5 * (KNOTS - 1) * FINE
@@ -29,11 +32,18 @@
 WIDE = (3 * SLOTS + 2) * SUB
 TALL = PASSES * OUTPUTS * SUB
 STAGED = 4
+ORDER = ((("far", 0), ("far", 1), ("far", 2), ("far", 3), ("far", 4), ("far", 5), ("far", 6), ("far", 7), ("near", 0), ), (("hop", 0), ("hop", 1), ), (("hop", 2), ), (("near", 1), ("near", 2), ))
+HOPS = sum(kind == "hop" for part in ORDER for kind, _ in part)
+NEARS = sum(kind == "near" for part in ORDER for kind, _ in part)
 MESH = pl.DeviceIdType.MESH
 
 
 def rows_at(start):
     return pl.ds(pl.multiple_of(start, SUB), SUB)
+
+
+def place_of(chunk):
+    return pl.multiple_of(SUB * (1 + chunk + chunk // LAST), SUB)
 
 
 def build_weights(lights, vectors, transfer, weights):
@@ -98,6 +108,12 @@
                     below = jnp.where(sub == s, pltpu.roll(line, s, 0), below)
             pack[rank, part * SUB : (part + 1) * SUB, :] = above
             pack[rank, SLAB + part * SUB : SLAB + (part + 1) * SUB, :] = below
+            middle = zero
+            for s in range(SUB):
+                line = slab[part * SUB + s, base + LAST * SUB : base + ROWS, :]
+                middle = jnp.where(sub == s, pltpu.roll(line, s, 0) if s else line, middle)
+            start = MIDDLE + part * SUB
+            pack[rank, start : start + SUB, :] = middle
 
 
 def pair(a, b):
@@ -122,9 +138,10 @@
     first = lane % CHUNKS == 0
     couple = pair(lane // 2, lane // 2)
     nothing = jnp.zeros((TWO, LANES), bf16)
-    here = rows_at(SUB + SUB * chunk)
-    above = pl.ds(SUB + SUB * chunk - 1, SUB)
-    below = pl.ds(SUB + SUB * chunk + 1, SUB)
+    start = place_of(chunk)
+    here = pl.ds(start, SUB)
+    above = pl.ds(start - 1, SUB)
+    below = pl.ds(start + 1, SUB)
     for source in range(RANKS):
         west = pltpu.roll(halo[source, 32:40, :], (LANES + 1 - chunk) % LANES, 1)
         east = pltpu.roll(halo[source, 40:48, :], (LANES - chunk) % LANES, 1)
@@ -238,10 +255,12 @@
 
 def kernel(
     tiles,
-    flips, lights, light_vectors, transfer, field,
+    flips_hbm, lights_hbm, vectors_hbm, transfer_hbm, field,
     out,
-    slab, volume, pack, left, right, halo, relay, pack_relay, draft, weights, shift, stage,
-    local_sem, col_send, col_recv, pack_send, pack_recv, pack_relay_recv, pack_forward,
+    flips, lights, light_vectors, transfer,
+    slab, volume, pack, left, right, halo, relay, pack_relay, draft, weights, shift, stage, image,
+    table_sem, local_sem, out_sem, col_send, col_recv,
+    pack_send, pack_recv, pack_far_send, pack_far_recv, pack_hop_send, pack_hop_recv,
     near_send, near_recv, far_send, far_recv, hop_send, hop_recv,
 ):
     rank = lax.axis_index("depth")
@@ -251,72 +270,97 @@
     sides = (ahead, behind)
     east, west = (tile + 1) % tiles, (tile + tiles - 1) % tiles
 
-    fetch = pltpu.make_async_copy(field, slab, local_sem.at[0])
-    fetch.start()
-    own = pltpu.make_async_copy(
-        field.at[:, pl.ds(pl.multiple_of(rank * ROWS, SUB), ROWS), :],
-        volume.at[pl.ds(1 + rank * SLAB, SLAB), pl.ds(SUB, ROWS), :],
-        local_sem.at[1],
-    )
-    own.start()
-
     barrier = pltpu.get_barrier_semaphore()
     for where in sides:
         pl.semaphore_signal(barrier, inc=1, device_id=(where, tile), device_id_type=MESH)
-    for where in (east, west):
-        pl.semaphore_signal(barrier, inc=1, device_id=(rank, where), device_id_type=MESH)
+
+    fetch = pltpu.make_async_copy(field, slab, local_sem.at[0])
+    fetch.start()
+    own = [
+        pltpu.make_async_copy(
+            field.at[:, pl.ds(pl.multiple_of(rank * ROWS + start, SUB), count), :],
+            volume.at[pl.ds(1 + rank * SLAB, SLAB), pl.ds(target, count), :],
+            local_sem.at[n],
+        )
+        for n, (start, count, target) in enumerate(
+            ((0, LAST * SUB, SUB), (LAST * SUB, SUB, (LAST + 2) * SUB)), start=1
+        )
+    ]
+    for copy in own:
+        copy.start()
+    tables = [
+        pltpu.make_async_copy(source, target, table_sem.at[n])
+        for n, (source, target) in enumerate(
+            ((flips_hbm, flips), (lights_hbm, lights), (vectors_hbm, light_vectors), (transfer_hbm, transfer))
+        )
+    ]
+    for copy in tables:
+        copy.start()
+
+    def greet():
+        for where in (east, west):
+            pl.semaphore_signal(barrier, inc=1, device_id=(rank, where), device_id_type=MESH)
+
+    greet()
     pl.semaphore_wait(barrier, 4)
 
-    def near(side, c):
+    def send(source, target, sent, received, side):
         return pltpu.make_async_remote_copy(
-            src_ref=field.at[:, rows_at(sides[side] * ROWS + c * SUB), :],
-            dst_ref=volume.at[pl.ds(1 + rank * SLAB, SLAB), rows_at(SUB + c * SUB), :],
-            send_sem=near_send.at[side, c],
-            recv_sem=near_recv.at[side, c],
+            src_ref=source,
+            dst_ref=target,
+            send_sem=sent,
+            recv_sem=received,
             device_id=(sides[side], tile),
             device_id_type=MESH,
         )
 
-    def far(side, c):
-        return pltpu.make_async_remote_copy(
-            src_ref=field.at[pl.ds(side * HALF, HALF), rows_at(across * ROWS + c * SUB), :],
-            dst_ref=relay.at[side, c],
-            send_sem=far_send.at[side, c],
-            recv_sem=far_recv.at[side, c],
-            device_id=(sides[side], tile),
-            device_id_type=MESH,
-        )
-
-    def hop(side, c):
+    def near_chunk(side, c):
+        return send(
+            field.at[:, rows_at(sides[side] * ROWS + c * SUB), :],
+            volume.at[pl.ds(1 + rank * SLAB, SLAB), pl.ds(place_of(c), SUB), :],
+            near_send.at[side], near_recv.at[side, c], side,
+        )
+
+    def far_chunk(side, c):
+        return send(
+            field.at[pl.ds(side * HALF, HALF), rows_at(across * ROWS + c * SUB), :],
+            relay.at[side, :, rows_at(c * SUB), :],
+            far_send.at[side], far_recv.at[side, c], side,
+        )
+
+    def hop_chunk(side, c):
         origin = sides[1 - side]
-        return pltpu.make_async_remote_copy(
-            src_ref=relay.at[side, c],
-            dst_ref=volume.at[
-                pl.ds(1 + origin * SLAB + side * HALF, HALF), rows_at(SUB + c * SUB), :
-            ],
-            send_sem=hop_send.at[side, c],
-            recv_sem=hop_recv.at[side, c],
-            device_id=(sides[side], tile),
-            device_id_type=MESH,
-        )
-
-    def launch(c, carry):
+        return send(
+            relay.at[side, :, rows_at(c * SUB), :],
+            volume.at[pl.ds(1 + origin * SLAB + side * HALF, HALF), pl.ds(place_of(c), SUB), :],
+            hop_send.at[side], hop_recv.at[side, c], side,
+        )
+
+    def both(build, c):
         for side in range(2):
-            far(side, c).start()
-        return carry
-
-    lax.fori_loop(0, CHUNKS, launch, 0)
-    for side in range(2):
-        near(side, 0).start()
-
-    zero_layer = jnp.zeros((ROWS + 2 * SUB, LANES), jnp.float32)
+            build(side, c).start()
+
+    def issue(order):
+        for kind, c in order:
+            if kind == "far":
+                both(far_chunk, c)
+            elif kind == "near":
+                both(near_chunk, c)
+            else:
+                relay_on(c)
+
+    def relay_on(c):
+        for side in range(2):
+            far_chunk(side, c).wait_recv()
+            hop_chunk(side, c).start()
+
+    issue(ORDER[0])
+
+    zero_layer = jnp.zeros((TOTAL, LANES), jnp.float32)
     volume[0] = zero_layer
     volume[DEPTH + 1] = zero_layer
     fetch.wait()
     pack_borders(tile, tiles, slab, pack, left, right)
-    build_weights(lights, light_vectors, transfer, draft)
-    weights[...] = draft[...].astype(jnp.bfloat16)
-    build_shift(shift)
 
     columns = [
         pltpu.make_async_remote_copy(
@@ -329,63 +373,65 @@
         )
         for n, (source, start, where) in enumerate(((right, 32, east), (left, 40, west)))
     ]
+
     for copy in columns:
         copy.start()
-    own.wait()
+    for copy in tables:
+        copy.wait()
+    build_weights(lights, light_vectors, transfer, draft)
+    weights[...] = draft[...].astype(jnp.bfloat16)
+    build_shift(shift)
+    for copy in own:
+        copy.wait()
+    issue(ORDER[1])
     for copy in columns:
         copy.wait_recv()
 
-    packs = [
-        pltpu.make_async_remote_copy(
-            src_ref=pack.at[sides[side]],
-            dst_ref=halo.at[rank],
-            send_sem=pack_send.at[side],
-            recv_sem=pack_recv.at[side],
-            device_id=(sides[side], tile),
-            device_id_type=MESH,
+    part = PACK // 2
+    pack_far = [
+        send(
+            pack.at[across, side * part : (side + 1) * part, :],
+            pack_relay.at[side],
+            pack_far_send.at[side], pack_far_recv.at[side], side,
         )
         for side in range(2)
     ]
-    packs.append(
-        pltpu.make_async_remote_copy(
-            src_ref=pack.at[across],
-            dst_ref=pack_relay,
-            send_sem=pack_send.at[2],
-            recv_sem=pack_relay_recv,
-            device_id=(ahead, tile),
-            device_id_type=MESH,
-        )
-    )
-    packs[2].start()
-    packs[0].start()
-    packs[1].start()
-    mine = pltpu.make_async_copy(pack.at[rank], halo.at[rank], local_sem.at[2])
+    pack_near = [
+        send(pack.at[sides[side]], halo.at[rank], pack_send.at[side], pack_recv.at[side], side)
+        for side in range(2)
+    ]
+    pack_hop = [
+        send(
+            pack_relay.at[side],
+            halo.at[sides[1 - side], side * part : (side + 1) * part, :],
+            pack_hop_send.at[side], pack_hop_recv.at[side], side,
+        )
+        for side in range(2)
+    ]
+    for copy in pack_far + pack_near:
+        copy.start()
+    mine = pltpu.make_async_copy(pack.at[rank], halo.at[rank], local_sem.at[3])
     mine.start()
-    packs[2].wait_recv()
-    forward = pltpu.make_async_remote_copy(
-        src_ref=pack_relay,
-        dst_ref=halo.at[behind],
-        send_sem=pack_forward.at[0],
-        recv_sem=pack_forward.at[1],
-        device_id=(ahead, tile),
-        device_id_type=MESH,
-    )
-    forward.start()
+    issue(ORDER[2])
+    for side in range(2):
+        pack_far[side].wait_recv()
+        pack_hop[side].start()
+    issue(ORDER[3])
     mine.wait()
-    packs[0].wait_recv()
-    packs[1].wait_recv()
-    forward.wait_recv()
-
-    def expand(d, carry):
-        source = d // SLAB
-        line = d % SLAB
-        volume[d + 1, 0:SUB, :] = jnp.broadcast_to(halo[source, pl.ds(line, 1), :], (SUB, LANES))
-        volume[d + 1, SUB + ROWS : ROWS + 2 * SUB, :] = jnp.broadcast_to(
-            halo[source, pl.ds(SLAB + line, 1), :], (SUB, LANES)
-        )
-        return carry
-
-    lax.fori_loop(0, DEPTH, expand, 0)
+    for side in range(2):
+        pack_near[side].wait_recv()
+    for side in range(2):
+        pack_hop[side].wait_recv()
+
+    for d in range(DEPTH):
+        source, line = d // SLAB, d % SLAB
+        volume[d + 1, 0:SUB, :] = jnp.broadcast_to(halo[source, line : line + 1, :], (SUB, LANES))
+        volume[d + 1, TOTAL - SUB : TOTAL, :] = jnp.broadcast_to(
+            halo[source, SLAB + line : SLAB + line + 1, :], (SUB, LANES)
+        )
+        volume[d + 1, ROWS : ROWS + SUB, :] = jnp.broadcast_to(
+            halo[source, MIDDLE + line : MIDDLE + line + 1, :], (SUB, LANES)
+        )
 
     flip = flips[0]
 
@@ -393,82 +439,93 @@
         prepare(chunk, volume, halo, shift, stage)
 
         def write(p, c, value):
-            out[p, c, rows_at(chunk * SUB), :] = value
+            image[p, c, rows_at(chunk * SUB), :] = value
 
         shade(flip, weights, stage, write)
-
-    def relay_on(c):
+        pltpu.make_async_copy(
+            image.at[:, :, rows_at(chunk * SUB), :], out.at[:, :, rows_at(chunk * SUB), :], out_sem
+        ).start()
+
+    def arrive(c):
         for side in range(2):
-            far(side, c).wait_recv()
-            hop(side, c).start()
-
-    relay_on(0)
-    relay_on(1)
-    for side in range(2):
-        near(side, 1).start()
+            near_chunk(side, c).wait_recv()
+            hop_chunk(side, c).wait_recv()
 
     def advance(c, carry):
-        @pl.when(c < CHUNKS - 2)
+        @pl.when(c < CHUNKS - HOPS)
         def _():
-            relay_on(c + 2)
-            for side in range(2):
-                near(side, c + 2).start()
-
-        @pl.when(c < CHUNKS)
+            relay_on(c + HOPS)
+
+        @pl.when(c < CHUNKS - NEARS)
         def _():
-            for side in range(2):
-                near(side, c).wait_recv()
-                hop(side, c).wait_recv()
+            both(near_chunk, c + NEARS)
+
+        @pl.when(c < LAST)
+        def _():
+            arrive(c)
 
         @pl.when(c > 0)
         def _():
             compute(c - 1)
 
+        @pl.when(c == LAST)
+        def _():
+            arrive(c)
+            for d in range(DEPTH):
+                volume[d + 1, ROWS + SUB - 1 : ROWS + SUB, :] = volume[d + 1, ROWS - 1 : ROWS, :]
+
         return carry
 
     lax.fori_loop(0, CHUNKS + 1, advance, 0)
 
-    def drain(c, carry):
-        for side in range(2):
-            near(side, c).wait_send()
-            far(side, c).wait_send()
-            hop(side, c).wait_send()
-        return carry
-
-    lax.fori_loop(0, CHUNKS, drain, 0)
-    for copy in columns + packs + [forward]:
+    for side in range(2):
+        send(
+            field.at[:, pl.ds(pl.multiple_of(sides[side] * ROWS, SUB), ROWS), :],
+            volume.at[pl.ds(1 + rank * SLAB, SLAB), pl.ds(SUB, ROWS), :],
+            near_send.at[side], near_recv.at[side, 0], side,
+        ).wait_send()
+        for sent in (far_send, hop_send):
+            send(
+                relay.at[side], relay.at[side], sent.at[side], far_recv.at[side, 0], side
+            ).wait_send()
+    for copy in columns + pack_far + pack_near + pack_hop:
         copy.wait_send()
+    pltpu.make_async_copy(image, out, out_sem).wait()
 
 
 def solution(mesh):
     tiles = mesh.shape["tile"]
 
     def on_device(field, light_vectors, transfer, light_index, flips):
-        smem = pl.BlockSpec(memory_space=pltpu.SMEM)
-        vmem = pl.BlockSpec(memory_space=pltpu.VMEM)
+        anywhere = pl.BlockSpec(memory_space=pl.ANY)
         dma = pltpu.SemaphoreType.DMA
-        f32 = jnp.float32
+        f32, i32 = jnp.float32, jnp.int32
         return pl.pallas_call(
             functools.partial(kernel, tiles),
-            out_shape=jax.ShapeDtypeStruct((PASSES, CHANNELS, ROWS, LANES), f32),
-            in_specs=[smem, smem, smem, smem, pl.BlockSpec(memory_space=pl.ANY)],
-            out_specs=vmem,
+            out_shape=pltpu.VMEM((PASSES, CHANNELS, ROWS, LANES), f32),
+            in_specs=[anywhere] * 5,
+            out_specs=anywhere,
             scratch_shapes=[
+                pltpu.SMEM(flips.shape, i32),
+                pltpu.SMEM(light_index.shape, i32),
+                pltpu.SMEM(light_vectors.shape[::-1], f32),
+                pltpu.SMEM((CHANNELS, KNOTS, transfer.shape[0]), f32),
                 pltpu.VMEM((SLAB, RANKS * ROWS, LANES), f32),
-                pltpu.VMEM((DEPTH + 2, ROWS + 2 * SUB, LANES), f32),
+                pltpu.VMEM((DEPTH + 2, TOTAL, LANES), f32),
                 pltpu.VMEM((RANKS, PACK, LANES), f32),
                 pltpu.VMEM((RANKS, SUB, LANES), f32),
                 pltpu.VMEM((RANKS, SUB, LANES), f32),
                 pltpu.VMEM((RANKS, PACK, LANES), f32),
-                pltpu.VMEM((2, CHUNKS, HALF, SUB, LANES), f32),
-                pltpu.VMEM((PACK, LANES), f32),
+                pltpu.VMEM((2, HALF, ROWS, LANES), f32),
+                pltpu.VMEM((2, PACK // 2, LANES), f32),
                 pltpu.VMEM((TALL, WIDE), f32),
                 pltpu.VMEM((TALL, WIDE), jnp.bfloat16),
                 pltpu.VMEM((4 * LANES, LANES), jnp.bfloat16),
                 pltpu.VMEM((DEPTH, STAGED, SUB, LANES), f32),
-                dma((3,)), dma((2,)), dma((2,)), dma((3,)), dma((2,)), dma, dma((2,)),
-                dma((2, CHUNKS)), dma((2, CHUNKS)), dma((2, CHUNKS)),
-                dma((2, CHUNKS)), dma((2, CHUNKS)), dma((2, CHUNKS)),
+                pltpu.VMEM((PASSES, CHANNELS, ROWS, LANES), f32),
+                dma((4,)), dma((4,)), dma, dma((2,)), dma((2,)),
+                dma((2,)), dma((2,)), dma((2,)), dma((2,)), dma((2,)), dma((2,)),
+                dma((2,)), dma((2, CHUNKS)), dma((2,)), dma((2, CHUNKS)), dma((2,)), dma((2, CHUNKS)),
             ],
             compiler_params=pltpu.CompilerParams(collective_id=0, has_side_effects=True),
             name="render",

time: 44.6 us -> 36.7 us (0.82)
  Pallas kernels: 41.9 us -> 35.1 us
  local copies, waits for them, and re-layouts: 1.89 us -> 0.8 us
    pallas_call x1, Pallas kernels: 41.9 us -> 35.1 us  [on_device(): pl.pallas_call(functools.partial(kernel, tiles), out_shape=pltpu.VMEM((PA...]
    unnamed x1, local copies, waits for them, and re-layouts: 1.89 us -> 0.8 us
where the time goes in v2:
time: 36.7 us; the launch traced here: 36.6 us
  Pallas kernels  35.1 us (96%)
  local copies, waits for them, and re-layouts  0.8 us (2%)
  between operations  0.66 us (2%)
    pallas_call x1, Pallas kernels, on_device(): pl.pallas_call(functools.partial(kernel, tiles), out_shape=pltpu.VMEM((PA...  35.1 us
    unnamed x1, local copies, waits for them, and re-layouts  0.8 us

profile of v2, /device:TPU:8, one launch (start us, length us, event | category | flops | bytes accessed | tf_op | source)
XLA Modules:
  0.0 36.6 jit_solution(4147719674405428986)
XLA Ops:
  0.7 35.1 %render.1 = f32[4,4,64,128]{3,2,1,0:T(8,128)S(1)} custom-call(s32[1]{0:T(128)S(6)} %copy.8.flips_hbm, s32[4]{0:T(128)} %lights_hbm.1, f32[3,16]{1,0:T(4,128)} %bitcast.3, f32[4,8,16]{2,1,0:T(8,128)} %bitcast.2, f32[16,256,128]{2,1,0:T(8,128)} %field.1), custom_call_target="tpu_custom_call" | custom-call | tf_op jit(solution)/shard_map/render/pallas_call | solution.py:503
  35.8 0.8 %copy.7 = f32[4,4,64,128]{3,2,1,0:T(8,128)} copy(f32[4,4,64,128]{3,2,1,0:T(8,128)S(1)} %render.1) | data formatting | bytes 1048576

commit v3 on v2

--- a/solution.py
+++ b/solution.py
@@ -32,7 +32,7 @@
 WIDE = (3 * SLOTS + 2) * SUB
 TALL = PASSES * OUTPUTS * SUB
 STAGED = 4
-ORDER = ((("far", 0), ("far", 1), ("far", 2), ("far", 3), ("far", 4), ("far", 5), ("far", 6), ("far", 7), ("near", 0), ), (("hop", 0), ("hop", 1), ), (("hop", 2), ), (("near", 1), ("near", 2), ))
+ORDER = ((("far", 0), ("far", 1), ("far", 2), ("far", 3), ("far", 4), ("far", 5), ("far", 6), ("far", 7), ("near", 0), ), (("hop", 0), ("hop", 1), ), (("hop", 2), ("near", 1), ), (("near", 2), ))
 HOPS = sum(kind == "hop" for part in ORDER for kind, _ in part)
 NEARS = sum(kind == "near" for part in ORDER for kind, _ in part)
 MESH = pl.DeviceIdType.MESH
@@ -258,8 +258,8 @@
     flips_hbm, lights_hbm, vectors_hbm, transfer_hbm, field,
     out,
     flips, lights, light_vectors, transfer,
-    slab, volume, pack, left, right, halo, relay, pack_relay, draft, weights, shift, stage, image,
-    table_sem, local_sem, out_sem, col_send, col_recv,
+    slab, volume, pack, left, right, halo, relay, pack_relay, draft, weights, shift, stage,
+    table_sem, local_sem, col_send, col_recv,
     pack_send, pack_recv, pack_far_send, pack_far_recv, pack_hop_send, pack_hop_recv,
     near_send, near_recv, far_send, far_recv, hop_send, hop_recv,
 ):
@@ -439,12 +439,9 @@
         prepare(chunk, volume, halo, shift, stage)
 
         def write(p, c, value):
-            image[p, c, rows_at(chunk * SUB), :] = value
+            out[p, c, rows_at(chunk * SUB), :] = value
 
         shade(flip, weights, stage, write)
-        pltpu.make_async_copy(
-            image.at[:, :, rows_at(chunk * SUB), :], out.at[:, :, rows_at(chunk * SUB), :], out_sem
-        ).start()
 
     def arrive(c):
         for side in range(2):
@@ -470,9 +467,15 @@
 
         @pl.when(c == LAST)
         def _():
-            arrive(c)
             for d in range(DEPTH):
                 volume[d + 1, ROWS + SUB - 1 : ROWS + SUB, :] = volume[d + 1, ROWS - 1 : ROWS, :]
+            for side in range(2):
+                send(
+                    relay.at[side], relay.at[side], far_send.at[side], far_recv.at[side, 0], side
+                ).wait_send()
+            for copy in columns + pack_far + pack_near + pack_hop:
+                copy.wait_send()
+            arrive(c)
 
         return carry
 
@@ -484,13 +487,9 @@
             volume.at[pl.ds(1 + rank * SLAB, SLAB), pl.ds(SUB, ROWS), :],
             near_send.at[side], near_recv.at[side, 0], side,
         ).wait_send()
-        for sent in (far_send, hop_send):
-            send(
-                relay.at[side], relay.at[side], sent.at[side], far_recv.at[side, 0], side
-            ).wait_send()
-    for copy in columns + pack_far + pack_near + pack_hop:
-        copy.wait_send()
-    pltpu.make_async_copy(image, out, out_sem).wait()
+        send(
+            relay.at[side], relay.at[side], hop_send.at[side], far_recv.at[side, 0], side
+        ).wait_send()
 
 
 def solution(mesh):
@@ -504,7 +503,7 @@
             functools.partial(kernel, tiles),
             out_shape=pltpu.VMEM((PASSES, CHANNELS, ROWS, LANES), f32),
             in_specs=[anywhere] * 5,
-            out_specs=anywhere,
+            out_specs=pl.BlockSpec(memory_space=pltpu.VMEM),
             scratch_shapes=[
                 pltpu.SMEM(flips.shape, i32),
                 pltpu.SMEM(light_index.shape, i32),
@@ -522,8 +521,7 @@
                 pltpu.VMEM((TALL, WIDE), jnp.bfloat16),
                 pltpu.VMEM((4 * LANES, LANES), jnp.bfloat16),
                 pltpu.VMEM((DEPTH, STAGED, SUB, LANES), f32),
-                pltpu.VMEM((PASSES, CHANNELS, ROWS, LANES), f32),
-                dma((4,)), dma((4,)), dma, dma((2,)), dma((2,)),
+                dma((4,)), dma((4,)), dma((2,)), dma((2,)),
                 dma((2,)), dma((2,)), dma((2,)), dma((2,)), dma((2,)), dma((2,)),
                 dma((2,)), dma((2, CHUNKS)), dma((2,)), dma((2, CHUNKS)), dma((2,)), dma((2, CHUNKS)),
             ],

time: 36.7 us -> 36.3 us (0.989)
  no operation moved by 1% of the time
where the time goes in v3:
time: 36.3 us; the launch traced here: 36.2 us
  Pallas kernels  34.8 us (96%)
  local copies, waits for them, and re-layouts  0.8 us (2%)
  between operations  0.66 us (2%)
    pallas_call x1, Pallas kernels, on_device(): pl.pallas_call(functools.partial(kernel, tiles), out_shape=pltpu.VMEM((PA...  34.8 us
    unnamed x1, local copies, waits for them, and re-layouts  0.8 us

profile of v3, /device:TPU:8, one launch (start us, length us, event | category | flops | bytes accessed | tf_op | source)
XLA Modules:
  0.0 36.2 jit_solution(526913031667179457)
XLA Ops:
  0.7 34.8 %render.1 = f32[4,4,64,128]{3,2,1,0:T(8,128)S(1)} custom-call(s32[1]{0:T(128)S(6)} %copy.8.flips_hbm, s32[4]{0:T(128)} %lights_hbm.1, f32[3,16]{1,0:T(4,128)} %bitcast.3, f32[4,8,16]{2,1,0:T(8,128)} %bitcast.2, f32[16,256,128]{2,1,0:T(8,128)} %field.1), custom_call_target="tpu_custom_call" | custom-call | tf_op jit(solution)/shard_map/render/pallas_call | solution.py:502
  35.4 0.8 %copy.7 = f32[4,4,64,128]{3,2,1,0:T(8,128)} copy(f32[4,4,64,128]{3,2,1,0:T(8,128)S(1)} %render.1) | data formatting | bytes 1048576

commit v4 on v3

--- a/solution.py
+++ b/solution.py
@@ -19,7 +19,8 @@
 ROWS = 64
 CHUNKS = ROWS // SUB
 HALF = SLAB // 2
-STEP = 64
+INNER = SLAB - 2
+OUTER = DEPTH - INNER
 PACK = 64
 LAST = CHUNKS - 1
 MIDDLE = 48
@@ -132,7 +133,7 @@
         shift[n * LANES : (n + 1) * LANES, :] = part.astype(jnp.bfloat16)
 
 
-def prepare(chunk, volume, halo, shift, stage):
+def prepare(chunk, slabs, first_layer, layers, volume, shift, stage):
     lane = lax.broadcasted_iota(jnp.int32, (SUB, LANES), 1)
     bf16 = jnp.bfloat16
     first = lane % CHUNKS == 0
@@ -142,21 +143,22 @@
     here = pl.ds(start, SUB)
     above = pl.ds(start - 1, SUB)
     below = pl.ds(start + 1, SUB)
-    for source in range(RANKS):
-        west = pltpu.roll(halo[source, 32:40, :], (LANES + 1 - chunk) % LANES, 1)
-        east = pltpu.roll(halo[source, 40:48, :], (LANES - chunk) % LANES, 1)
+    for source, halo in slabs:
+        west = pltpu.roll(halo[32:40, :], (LANES + 1 - chunk) % LANES, 1)
+        east = pltpu.roll(halo[40:48, :], (LANES - chunk) % LANES, 1)
         border = jnp.where(first, east, west)
         border_top = pair(border, border)
         rest = border - border_top[:SUB].astype(jnp.float32)
         border_low = pair(rest, rest)
         rows = []
-        for two in range(SLAB // 2):
-            d = source * SLAB + 2 * two
+        for two in range(layers // 2):
+            layer = first_layer + 2 * two
+            d = source * SLAB + layer
             x = jnp.concatenate([volume[d + 1, here, :], volume[d + 2, here, :]], axis=0)
             top = x.astype(bf16)
             low = (x - top.astype(jnp.float32)).astype(bf16)
             wanted = jnp.concatenate(
-                [jnp.full((SUB, LANES), float((2 * two + n) * CHUNKS // 2), jnp.float32) for n in range(2)],
+                [jnp.full((SUB, LANES), float((layer + n) * CHUNKS // 2), jnp.float32) for n in range(2)],
                 axis=0,
             ).astype(bf16)
             mask = couple == wanted
@@ -169,8 +171,8 @@
         across = jnp.dot(
             jnp.concatenate(rows, axis=0), shift[...], preferred_element_type=jnp.float32
         )
-        for u in range(SLAB):
-            d = source * SLAB + u
+        for u in range(layers):
+            d = source * SLAB + first_layer + u
             dx = across[u * SUB : (u + 1) * SUB, :]
             dz = volume[d + 2, here, :] - volume[d, here, :]
             dy = volume[d + 1, below, :] - volume[d + 1, above, :]
@@ -181,9 +183,7 @@
             stage[d, 3] = dz * scale
 
 
-def shade(flip, weights, stage, write):
-    start = flip * (DEPTH - 1)
-    sign = 1 - 2 * flip
+def shade(places, weights, stage, insert):
     bf16 = jnp.bfloat16
 
     def levels(values):
@@ -197,11 +197,10 @@
     full2 = levels((FINE, FINE))
     ones = levels((1, 1))
 
-    def cells(step, state):
+    def cells(state):
         state = list(state)
         columns = []
-        for u in range(STEP):
-            at = start + sign * (step * STEP + u)
+        for at in places:
             place, nx, ny, nz = [stage[at, n] for n in range(STAGED)]
             level = jnp.floor(place)
             step_in = place - level
@@ -223,10 +222,11 @@
             ]
             top = ramp + [flat]
             columns.append(jnp.concatenate(top + top + fine + [flat_low, ones], axis=0))
-        for two in range(STEP // 2):
+        for two in range(len(places) // 2):
             moving = jnp.concatenate(columns[2 * two : 2 * two + 2], axis=1)
             mixed = jnp.dot(weights[...], moving, preferred_element_type=jnp.float32)
             for side in range(2):
+                state = insert(2 * two + side, state)
                 for p in range(PASSES):
                     red, green, blue, opacity, facing = [
                         mixed[
@@ -246,11 +246,7 @@
 
     zero = jnp.zeros((SUB, LANES), jnp.float32)
     one = jnp.ones((SUB, LANES), jnp.float32)
-    state = cells(0, tuple([zero, zero, zero, one] * PASSES))
-    for p in range(PASSES):
-        for c in range(3):
-            write(p, c, state[p * CHANNELS + c])
-        write(p, 3, 1.0 - state[p * CHANNELS + 3])
+    return cells([zero, zero, zero, one] * PASSES)
 
 
 def kernel(
@@ -258,7 +254,7 @@
     flips_hbm, lights_hbm, vectors_hbm, transfer_hbm, field,
     out,
     flips, lights, light_vectors, transfer,
-    slab, volume, pack, left, right, halo, relay, pack_relay, draft, weights, shift, stage,
+    slab, volume, pack, left, right, halo, relay, pack_relay, draft, weights, shift, stage, inner,
     table_sem, local_sem, col_send, col_recv,
     pack_send, pack_recv, pack_far_send, pack_far_recv, pack_hop_send, pack_hop_recv,
     near_send, near_recv, far_send, far_recv, hop_send, hop_recv,
@@ -413,6 +409,26 @@
     mine = pltpu.make_async_copy(pack.at[rank], halo.at[rank], local_sem.at[3])
     mine.start()
     issue(ORDER[2])
+    flip = flips[0]
+    sign = 1 - 2 * flip
+    for line in range(SLAB):
+        layer = 1 + rank * SLAB + line
+        for start, row in ((0, line), (TOTAL - SUB, SLAB + line), (ROWS, MIDDLE + line)):
+            volume[layer, start : start + SUB, :] = jnp.broadcast_to(
+                pack[rank, row : row + 1, :], (SUB, LANES)
+            )
+    for line in range(SLAB):
+        layer = 1 + rank * SLAB + line
+        volume[layer, ROWS + SUB - 1 : ROWS + SUB, :] = volume[layer, ROWS - 1 : ROWS, :]
+
+    def ahead_of_time(chunk, carry):
+        prepare(chunk, [(rank, pack.at[rank])], 1, INNER, volume, shift, stage)
+        places = [rank * SLAB + 1 + flip * (INNER - 1) + sign * n for n in range(INNER)]
+        for n, value in enumerate(shade(places, weights, stage, lambda _, state: state)):
+            inner[chunk, n] = value
+        return carry
+
+    lax.fori_loop(0, 4, ahead_of_time, 0)
     for side in range(2):
         pack_far[side].wait_recv()
         pack_hop[side].start()
@@ -429,19 +445,44 @@
         volume[d + 1, TOTAL - SUB : TOTAL, :] = jnp.broadcast_to(
             halo[source, SLAB + line : SLAB + line + 1, :], (SUB, LANES)
         )
-        volume[d + 1, ROWS : ROWS + SUB, :] = jnp.broadcast_to(
-            halo[source, MIDDLE + line : MIDDLE + line + 1, :], (SUB, LANES)
-        )
-
-    flip = flips[0]
+        volume[d + 1, ROWS : ROWS + SUB - 1, :] = jnp.broadcast_to(
+            halo[source, MIDDLE + line : MIDDLE + line + 1, :], (SUB - 1, LANES)
+        )
+
+    hits = [
+        jnp.full((SUB, LANES), jnp.where(flip == 1, RANKS - 1 - k, k), jnp.int32)
+        == jnp.full((SUB, LANES), rank, jnp.int32)
+        for k in range(RANKS)
+    ]
 
     def compute(chunk):
-        prepare(chunk, volume, halo, shift, stage)
-
-        def write(p, c, value):
-            out[p, c, rows_at(chunk * SUB), :] = value
-
-        shade(flip, weights, stage, write)
+        prepare(
+            chunk, [(n, halo.at[n]) for n in range(RANKS)], 0, SLAB, volume, shift, stage
+        )
+
+        places = []
+        for n in range(OUTER):
+            at = flip * (OUTER - 1) + sign * n
+            places.append(at + INNER * ((at + DEPTH - 1 - SLAB * rank) // DEPTH))
+
+        def insert(n, state):
+            if n % SLAB != 1:
+                return state
+            hit = hits[n // SLAB]
+            added = []
+            for p in range(PASSES):
+                base = p * CHANNELS
+                through = state[base + 3]
+                gain = jnp.where(hit, through, 0.0)
+                added += [state[base + c] + gain * inner[chunk, base + c] for c in range(3)]
+                added.append(jnp.where(hit, through * inner[chunk, base + 3], through))
+            return added
+
+        state = shade(places, weights, stage, insert)
+        for p in range(PASSES):
+            for c in range(3):
+                out[p, c, rows_at(chunk * SUB), :] = state[p * CHANNELS + c]
+            out[p, 3, rows_at(chunk * SUB), :] = 1.0 - state[p * CHANNELS + 3]
 
     def arrive(c):
         for side in range(2):
@@ -456,6 +497,10 @@
         @pl.when(c < CHUNKS - NEARS)
         def _():
             both(near_chunk, c + NEARS)
+
+        @pl.when(c < CHUNKS - 4)
+        def _():
+            ahead_of_time(c + 4, 0)
 
         @pl.when(c < LAST)
         def _():
@@ -521,6 +566,7 @@
                 pltpu.VMEM((TALL, WIDE), jnp.bfloat16),
                 pltpu.VMEM((4 * LANES, LANES), jnp.bfloat16),
                 pltpu.VMEM((DEPTH, STAGED, SUB, LANES), f32),
+                pltpu.VMEM((CHUNKS, PASSES * CHANNELS, SUB, LANES), f32),
                 dma((4,)), dma((4,)), dma((2,)), dma((2,)),
                 dma((2,)), dma((2,)), dma((2,)), dma((2,)), dma((2,)), dma((2,)),
                 dma((2,)), dma((2, CHUNKS)), dma((2,)), dma((2, CHUNKS)), dma((2,)), dma((2, CHUNKS)),

time: 36.3 us -> 35.6 us (0.981)
  Pallas kernels: 34.8 us -> 34.1 us
    pallas_call x1, Pallas kernels: 34.8 us -> 34.1 us  [on_device(): pl.pallas_call(functools.partial(kernel, tiles), out_shape=pltpu.VMEM((PA...]
where the time goes in v4:
time: 35.6 us; the launch traced here: 35.5 us
  Pallas kernels  34.1 us (96%)
  local copies, waits for them, and re-layouts  0.8 us (2%)
  between operations  0.66 us (2%)
    pallas_call x1, Pallas kernels, on_device(): pl.pallas_call(functools.partial(kernel, tiles), out_shape=pltpu.VMEM((PA...  34.1 us
    unnamed x1, local copies, waits for them, and re-layouts  0.8 us

profile of v4, /device:TPU:8, one launch (start us, length us, event | category | flops | bytes accessed | tf_op | source)
XLA Modules:
  0.0 35.5 jit_solution(13215511643925145321)
XLA Ops:
  0.7 34.1 %render.1 = f32[4,4,64,128]{3,2,1,0:T(8,128)S(1)} custom-call(s32[1]{0:T(128)S(6)} %copy.8.flips_hbm, s32[4]{0:T(128)} %lights_hbm.1, f32[3,16]{1,0:T(4,128)} %bitcast.3, f32[4,8,16]{2,1,0:T(8,128)} %bitcast.2, f32[16,256,128]{2,1,0:T(8,128)} %field.1), custom_call_target="tpu_custom_call" | custom-call | tf_op jit(solution)/shard_map/render/pallas_call | solution.py:547
  34.7 0.8 %copy.7 = f32[4,4,64,128]{3,2,1,0:T(8,128)} copy(f32[4,4,64,128]{3,2,1,0:T(8,128)S(1)} %render.1) | data formatting | bytes 1048576

commit v5 on v4

--- a/solution.py
+++ b/solution.py
@@ -26,7 +26,7 @@
 MIDDLE = 48
 TOTAL = ROWS + 3 * SUB
 TWO = 2 * SUB
-FINE = 32.0
+FINE = 256.0
 SPAN = 0.5 * (KNOTS - 1) * FINE
 SLOTS = KNOTS - 1 + 3
 OUTPUTS = CHANNELS + 1
@@ -190,8 +190,6 @@
         return jnp.concatenate([jnp.full((SUB, LANES), float(v), jnp.float32) for v in values], axis=0).astype(bf16)
 
     none = jnp.zeros((SUB, LANES), jnp.float32)
-    fine_ones = jnp.full((SUB, LANES), FINE, jnp.float32)
-    base = [levels((FINE * 2 * n, FINE * (2 * n + 1))) for n in range(4)]
     index = [levels((2 * n, 2 * n + 1 if n < 3 else 99)) for n in range(4)]
     zero2 = levels((0, 0))
     full2 = levels((FINE, FINE))
@@ -205,21 +203,20 @@
             level = jnp.floor(place)
             step_in = place - level
             floor_knot = jnp.floor(level * (1.0 / FINE))
-            whole, rest, knot = pair(level, level), pair(step_in, step_in), pair(floor_knot, floor_knot)
-            flat, deep, deep_full = pair(nx, ny), pair(none, nz), pair(fine_ones, nz)
+            within = level - floor_knot * FINE
+            whole, rest, knot = pair(within, within), pair(step_in, step_in), pair(floor_knot, floor_knot)
+            flat, deep = pair(nx, ny), pair(none, nz)
             flat_top, deep_top = flat.astype(jnp.float32), deep.astype(jnp.float32)
             flat_low = pair(nx - flat_top[:SUB], ny - flat_top[SUB:])
             deep_low = pair(none, nz - deep_top[SUB:])
+            inside = [knot == index[n] for n in range(4)]
             ramp = [
-                jnp.minimum(
-                    jnp.maximum(whole - base[n], zero2 if n < 3 else deep),
-                    full2 if n < 3 else deep_full,
+                jnp.where(
+                    inside[n], whole, jnp.where(knot > index[n], full2, zero2 if n < 3 else deep)
                 )
                 for n in range(4)
             ]
-            fine = [
-                jnp.where(knot == index[n], rest, zero2 if n < 3 else deep_low) for n in range(4)
-            ]
+            fine = [jnp.where(inside[n], rest, zero2 if n < 3 else deep_low) for n in range(4)]
             top = ramp + [flat]
             columns.append(jnp.concatenate(top + top + fine + [flat_low, ones], axis=0))
         for two in range(len(places) // 2):

time: 35.6 us -> 35.8 us (level)
  no operation moved by 1% of the time
where the time goes in v5:
time: 35.8 us; the launch traced here: 35.7 us
  Pallas kernels  34.3 us (96%)
  local copies, waits for them, and re-layouts  0.8 us (2%)
  between operations  0.66 us (2%)
    pallas_call x1, Pallas kernels, on_device(): pl.pallas_call(functools.partial(kernel, tiles), out_shape=pltpu.VMEM((PA...  34.3 us
    unnamed x1, local copies, waits for them, and re-layouts  0.8 us

profile of v5, /device:TPU:8, one launch (start us, length us, event | category | flops | bytes accessed | tf_op | source)
XLA Modules:
  0.0 35.7 jit_solution(17952017647416784605)
XLA Ops:
  0.7 34.3 %render.1 = f32[4,4,64,128]{3,2,1,0:T(8,128)S(1)} custom-call(s32[1]{0:T(128)S(6)} %copy.8.flips_hbm, s32[4]{0:T(128)} %lights_hbm.1, f32[3,16]{1,0:T(4,128)} %bitcast.3, f32[4,8,16]{2,1,0:T(8,128)} %bitcast.2, f32[16,256,128]{2,1,0:T(8,128)} %field.1), custom_call_target="tpu_custom_call" | custom-call | tf_op jit(solution)/shard_map/render/pallas_call | solution.py:544
  34.9 0.8 %copy.7 = f32[4,4,64,128]{3,2,1,0:T(8,128)} copy(f32[4,4,64,128]{3,2,1,0:T(8,128)S(1)} %render.1) | data formatting | bytes 1048576
